TPU v7x, 32 devices: a whole 2x2x4 slice. The times are simulated.
32 devices in a mesh: section: 2 (over x), dp: 16 (over z, y, core).
Axes of the slice: x: 2, y: 2, z: 4, core: 2. Of those that a mesh axis runs over, the one named last changes fastest.
Arguments:
- section_inputs: bfloat16 [2, 2048, 8192], P('section', 'dp'), may hold values from -6 to 6
- teacher_states: bfloat16 [2048, 8192], P('dp'), may hold values from -6 to 6
- confidence: int32 [2048], P('dp'), may hold values from 1 to 256
- gains: float32 [2, 8192], P('section'), may hold values from 0.1 to 1.9
- w_down: bfloat16 [2, 8192, 256], P('section', 'dp'), may hold values from -0.0625 to 0.0625
- w_up: bfloat16 [2, 8192, 256], P('section', 'dp'), may hold values from -0.375 to 0.375
Outputs:
- input_grads: bfloat16 [2, 2048, 8192], P('section', 'dp')
- grad_down: float32 [2, 8192, 256], P('section', 'dp')
- grad_up: float32 [2, 8192, 256], P('section', 'dp')
- grad_gain: float32 [2, 8192], P('section', 'dp')
All inputs are finite; a program needn't handle non-finite values.
Results may differ from a plain program's by a relative error of at most 0.013.
Values may be sent and summed in bfloat16 or wider, within the bound.
No kernel may reach another device: no remote copies, remote signals or barrier semaphores. Data moves between devices by JAX's collectives and lax.ppermute only.
A program may use at most 64 MiB of HBM per device.

v0:
```python
import jax
import jax.numpy as jnp
from jax import lax
from jax.sharding import PartitionSpec as P

MICRO = 4
ROWS = 32
TOK_DEV = 128
EPSILON = 1e-05


def shifted(block, axis, distance):
    devices = range(lax.axis_size(axis))
    route = [(i - distance, i) for i in devices if i - distance in devices]
    return lax.ppermute(block, axis, route)


def write_rows(buffer, fresh, first_row, active_step):
    previous = lax.dynamic_slice_in_dim(buffer, first_row, fresh.shape[0], 0)
    return lax.dynamic_update_slice_in_dim(
        buffer, jnp.where(active_step, fresh, previous), first_row, 0
    )


def local(section_inputs, teacher_states, confidence, gains, w_down, w_up):
    sections = lax.axis_size("section")
    section_index = lax.axis_index("section")
    layer_inputs = section_inputs[0]
    gain = gains[0]
    down_matrix, up_matrix = (
        lax.all_gather(w_down[0], "dp", axis=0, tiled=True),
        lax.all_gather(w_up[0], "dp", axis=0, tiled=True),
    )
    is_last = section_index == sections - 1
    rank_width = down_matrix.shape[1]
    width = down_matrix.shape[0]

    def run_step(step_index, carry):
        incoming, scaled_all, cot_all, pre_all, hidden_all, grads_all, gain_term = carry
        micro_index = step_index - (sections - 1 - section_index)
        active_step = (micro_index >= 0) & (micro_index < MICRO)
        first_row = jnp.clip(micro_index, 0, MICRO - 1) * ROWS
        rows_in = lax.dynamic_slice_in_dim(layer_inputs, first_row, ROWS, 0)
        teacher_rows = lax.dynamic_slice_in_dim(teacher_states, first_row, ROWS, 0)
        weight_rows = (
            lax.dynamic_slice_in_dim(confidence, first_row, ROWS, 0).astype(jnp.float32) / 256.0
        )
        values = rows_in.astype(jnp.float32)
        inverse = lax.rsqrt(jnp.mean(values * values, axis=-1, keepdims=True) + EPSILON)
        normed = values * inverse
        scaled = (normed * gain).astype(jnp.bfloat16)
        preact = jnp.dot(scaled, down_matrix, preferred_element_type=jnp.float32)
        hidden = jax.nn.silu(preact).astype(jnp.bfloat16)
        branch = jnp.einsum("tr,dr->td", hidden, up_matrix, preferred_element_type=jnp.float32)
        top_grad = (
            weight_rows[:, None] * (values + branch - teacher_rows.astype(jnp.float32))
        ).astype(jnp.bfloat16)
        cotangent = jnp.where(is_last, top_grad, incoming)
        hidden_grad = jnp.dot(cotangent, up_matrix, preferred_element_type=jnp.float32)
        sigmoid_val = jax.nn.sigmoid(preact)
        pre_grad = (hidden_grad * sigmoid_val * (1.0 + preact * (1.0 - sigmoid_val))).astype(
            jnp.bfloat16
        )
        normed_grad = jnp.einsum(
            "tr,dr->td", pre_grad, down_matrix, preferred_element_type=jnp.float32
        )
        scaled_grad = normed_grad * gain
        input_grad = cotangent.astype(jnp.float32) + inverse * (
            scaled_grad - normed * jnp.mean(scaled_grad * normed, axis=-1, keepdims=True)
        )
        input_grad = input_grad.astype(jnp.bfloat16)
        gain_term = gain_term + jnp.where(active_step, jnp.sum(normed_grad * normed, axis=0), 0.0)
        scaled_all = write_rows(scaled_all, scaled, first_row, active_step)
        cot_all = write_rows(cot_all, cotangent, first_row, active_step)
        pre_all = write_rows(pre_all, pre_grad, first_row, active_step)
        hidden_all = write_rows(hidden_all, hidden, first_row, active_step)
        grads_all = write_rows(grads_all, input_grad, first_row, active_step)
        outgoing = shifted(input_grad, "section", -1)
        return (outgoing, scaled_all, cot_all, pre_all, hidden_all, grads_all, gain_term)

    token_count = layer_inputs.shape[0]
    start_carry = (
        jnp.zeros((ROWS, width), jnp.bfloat16),
        jnp.zeros((token_count, width), jnp.bfloat16),
        jnp.zeros((token_count, width), jnp.bfloat16),
        jnp.zeros((token_count, rank_width), jnp.bfloat16),
        jnp.zeros((token_count, rank_width), jnp.bfloat16),
        jnp.zeros((token_count, width), jnp.bfloat16),
        jnp.zeros((width,), jnp.float32),
    )
    final_carry = lax.fori_loop(0, MICRO + sections - 1, run_step, start_carry)
    _, scaled_all, cot_all, pre_all, hidden_all, grads_all, gain_term = final_carry
    down_part = jnp.einsum("td,tr->dr", scaled_all, pre_all, preferred_element_type=jnp.float32)
    up_part = jnp.einsum("td,tr->dr", cot_all, hidden_all, preferred_element_type=jnp.float32)
    stacked = lax.psum_scatter(
        jnp.concatenate([down_part, up_part], axis=1).astype(jnp.bfloat16),
        "dp",
        scatter_dimension=0,
        tiled=True,
    ).astype(jnp.float32)
    gain_sum = lax.psum_scatter(gain_term, "dp", scatter_dimension=0, tiled=True)
    stacked = stacked / TOK_DEV
    grad_down = stacked[:, :rank_width]
    grad_up = stacked[:, rank_width:]
    return (grads_all[None], grad_down[None], grad_up[None], (gain_sum / TOK_DEV)[None])


def solution(mesh):
    in_specs = (
        P("section", "dp", None),
        P("dp", None),
        P("dp"),
        P("section", None),
        P("section", "dp", None),
        P("section", "dp", None),
    )
    out_specs = (
        P("section", "dp", None),
        P("section", "dp", None),
        P("section", "dp", None),
        P("section", "dp"),
    )
    return jax.shard_map(local, mesh=mesh, in_specs=in_specs, out_specs=out_specs, check_vma=False)
```

profile of v0, /device:TPU:0, one launch (start us, length us, event | category | flops | bytes accessed | tf_op | source)
XLA Modules:
  0.0 383.3 jit_solution(15505079731274536532)
XLA Ops:
  8.7 54.7 %all-gather.5.cloned.1.call-done = bf16[1,8192,256]{2,1,0:T(8,128)(2,1)} async-done(((bf16[1,512,256]{2,1,0:T(8,128)(2,1)}), bf16[1,8192,256]{2,1,0:T(8,128)(2,1)}) %all-gather.5.cloned.1.call-update) | async-done | bytes 4194320 | tf_op jit(solution)/shard_map/all_gather | solution.py:31
  63.5 51.2 %all-gather.7.cloned.1.call-done = bf16[1,8192,256]{2,1,0:T(8,128)(2,1)} async-done(((bf16[1,512,256]{2,1,0:T(8,128)(2,1)}), bf16[1,8192,256]{2,1,0:T(8,128)(2,1)}) %all-gather.7.cloned.1.call-update) | async-done | bytes 4194320 | tf_op jit(solution)/shard_map/all_gather | solution.py:32
  114.8 1.5 broadcast.67.clone.1
  116.3 1.5 broadcast.67.clone
  117.8 1.5 broadcast.67
  119.3 135.4 %while.28 = (s32[]{:T(128)}, bf16[32,8192]{1,0:T(8,128)(2,1)S(1)}, bf16[128,8192]{1,0:T(8,128)(2,1)}, bf16[128,8192]{1,0:T(8,128)(2,1)}, bf16[128,256]{1,0:T(8,1...) while((s32[]{:T(128)}, bf16[32,8192]{1,0:T(8,128)(2,1)S(1)}, ...), condition=%wide.region_4.5_spmd.clone, body=%wide.region_0.4_spmd.clone.sunk | while | flops 546234496 | bytes 63868848 | solution.py:91
  119.7 3.2 select_dynamic-update-slice_fusion.8
  123.1 2.4 fusion.48
  126.4 1.3 copy-done
  127.7 1.5 fusion.49
  129.2 3.0 select_dynamic-update-slice_fusion.10
  132.2 1.3 collective-permute-start
  133.5 14.7 %collective-permute-done = bf16[32,8192]{1,0:T(8,128)(2,1)S(1)} collective-permute-done((bf16[32,8192]{1,0:T(8,128)(2,1)S(1)}, bf16[32,8192]{1,0:T(8,128)(2,1)S(1)}, u32[]{:S(2)}, u32[]{:S(2)}) %collective-permute-start) | collective-permute-done | bytes 524320 | tf_op jit(solution)/shard_map/while/body/eval_jaxpr/ppermute | solution.py:15
  148.5 3.2 select_dynamic-update-slice_fusion.8
  152.0 2.4 fusion.48
  155.2 1.3 copy-done
  156.6 1.5 fusion.49
  158.1 3.0 select_dynamic-update-slice_fusion.10
  161.1 1.3 collective-permute-start
  162.4 13.8 %collective-permute-done = bf16[32,8192]{1,0:T(8,128)(2,1)S(1)} collective-permute-done((bf16[32,8192]{1,0:T(8,128)(2,1)S(1)}, bf16[32,8192]{1,0:T(8,128)(2,1)S(1)}, u32[]{:S(2)}, u32[]{:S(2)}) %collective-permute-start) | collective-permute-done | bytes 524320 | tf_op jit(solution)/shard_map/while/body/eval_jaxpr/ppermute | solution.py:15
  176.6 3.2 select_dynamic-update-slice_fusion.8
  180.0 2.4 fusion.48
  183.3 1.3 copy-done
  184.6 1.5 fusion.49
  186.1 3.0 select_dynamic-update-slice_fusion.10
  189.1 1.3 collective-permute-start
  190.4 12.9 %collective-permute-done = bf16[32,8192]{1,0:T(8,128)(2,1)S(1)} collective-permute-done((bf16[32,8192]{1,0:T(8,128)(2,1)S(1)}, bf16[32,8192]{1,0:T(8,128)(2,1)S(1)}, u32[]{:S(2)}, u32[]{:S(2)}) %collective-permute-start) | collective-permute-done | bytes 524320 | tf_op jit(solution)/shard_map/while/body/eval_jaxpr/ppermute | solution.py:15
  203.7 3.2 select_dynamic-update-slice_fusion.8
  207.1 2.4 fusion.48
  210.4 1.3 copy-done
  211.7 1.5 fusion.49
  213.2 3.0 select_dynamic-update-slice_fusion.10
  216.2 1.3 collective-permute-start
  217.5 12.0 %collective-permute-done = bf16[32,8192]{1,0:T(8,128)(2,1)S(1)} collective-permute-done((bf16[32,8192]{1,0:T(8,128)(2,1)S(1)}, bf16[32,8192]{1,0:T(8,128)(2,1)S(1)}, u32[]{:S(2)}, u32[]{:S(2)}) %collective-permute-start) | collective-permute-done | bytes 524320 | tf_op jit(solution)/shard_map/while/body/eval_jaxpr/ppermute | solution.py:15
  229.8 3.2 select_dynamic-update-slice_fusion.8
  233.3 2.4 fusion.48
  236.5 1.3 copy-done
  237.9 1.5 fusion.49
  239.3 3.0 select_dynamic-update-slice_fusion.10
  242.4 1.3 collective-permute-start
  243.7 11.1 %collective-permute-done = bf16[32,8192]{1,0:T(8,128)(2,1)S(1)} collective-permute-done((bf16[32,8192]{1,0:T(8,128)(2,1)S(1)}, bf16[32,8192]{1,0:T(8,128)(2,1)S(1)}, u32[]{:S(2)}, u32[]{:S(2)}) %collective-permute-start) | collective-permute-done | bytes 524320 | tf_op jit(solution)/shard_map/while/body/eval_jaxpr/ppermute | solution.py:15
  254.8 5.0 %convolution_convert_fusion.1 = bf16[8192,256]{0,1:T(8,128)(2,1)} fusion(bf16[128,8192]{1,0:T(8,128)(2,1)} %get-tuple-element.369, bf16[128,256]{1,0:T(8,128)(2,1)S(1)} %get-tuple-element.370), kind=kOutput, calls=%fused_computation.36 | convolution fusion | flops 538968064 | bytes 6356992 | tf_op jit(solution)/shard_map/td,tr->dr/dot_general | solution.py:93
  259.7 3.2 convolution_convert_fusion
  263.0 7.7 %pad_maximum_fusion = bf16[8192,512]{0,1:T(8,128)(2,1)} fusion(bf16[8192,256]{0,1:T(8,128)(2,1)} %convolution_convert_fusion, bf16[8192,256]{0,1:T(8,128)(2,1)} %convolution_convert_fusion.1), kind=kLoop, calls=%fused_computation.37 | loop fusion | flops 16777216 | bytes 16777216 | tf_op jit(solution)/shard_map/concatenate | solution.py:96
  272.5 59.9 %all-reduce = f32[8192]{0:T(1024)S(1)} all-reduce(f32[8192]{0:T(1024)S(1)} %get-tuple-element.373), channel_id=5, replica_groups=mesh['section'=2,'dp'=16] {'dp'}, use_global_device_ids=true, to_apply=%region_6.7.clone | all-reduce | flops 8192 | bytes 65536
  333.1 40.4 %reduce-scatter.2.cloned.1.call-done = bf16[512,512]{0,1:T(8,128)(2,1)} async-done(((bf16[8192,512]{0,1:T(8,128)(2,1)}), bf16[512,512]{0,1:T(8,128)(2,1)}) %reduce-scatter.2.cloned.1.call-update) | async-done | bytes 524304 | tf_op jit(solution)/shard_map/reduce_scatter | solution.py:95
  373.5 1.2 convert_multiply_fusion.3
  374.8 1.0 copy.13
  (69 shorter events, 11.4 us)
Async XLA Ops:
  7.2 56.3 %all-gather.5.cloned.1.call-start = ((), (), s32[]{:S(2)}) async-start(), calls=%async_computation.2 | async-start | bytes 4456448 | tf_op jit(solution)/shard_map/all_gather | solution.py:31
  7.9 106.8 %all-gather.7.cloned.1.call-start = ((), (), s32[]{:S(2)}) async-start(), calls=%async_computation.3 | async-start | bytes 4456448 | tf_op jit(solution)/shard_map/all_gather | solution.py:32
  8.6 364.9 %reduce-scatter.2.cloned.1.call-start = ((), (), s32[]{:S(2)}) async-start(), calls=%async_computation.1 | async-start | bytes 8912896 | tf_op jit(solution)/shard_map/reduce_scatter | solution.py:95
  116.3 3.0 copy-start.2
  116.3 3.0 copy-start.4
  116.3 3.0 copy-start.5
  119.7 3.5 copy-start.1
  125.6 2.2 copy-start
  132.2 16.0 %collective-permute-start = (bf16[32,8192]{1,0:T(8,128)(2,1)S(1)}, bf16[32,8192]{1,0:T(8,128)(2,1)S(1)}, u32[]{:S(2)}, u32[]{:S(2)}) collective-permute-start(bf16[32,8192]{1,0:T(8,128)(2,1)S(1)} %get-tuple-element.590), channel_id=1, source_target_pairs={{16,0},{17,1},{18,2},{19,3},{20,4},{21,5},{22,6},{23,7},{24,8},{25... | collective-permute-start | bytes 1572872 | tf_op jit(solution)/shard_map/while/body/eval_jaxpr/ppermute | solution.py:15
  148.5 3.5 copy-start.1
  154.4 2.2 copy-start
  161.1 15.2 %collective-permute-start = (bf16[32,8192]{1,0:T(8,128)(2,1)S(1)}, bf16[32,8192]{1,0:T(8,128)(2,1)S(1)}, u32[]{:S(2)}, u32[]{:S(2)}) collective-permute-start(bf16[32,8192]{1,0:T(8,128)(2,1)S(1)} %get-tuple-element.590), channel_id=1, source_target_pairs={{16,0},{17,1},{18,2},{19,3},{20,4},{21,5},{22,6},{23,7},{24,8},{25... | collective-permute-start | bytes 1572872 | tf_op jit(solution)/shard_map/while/body/eval_jaxpr/ppermute | solution.py:15
  176.5 3.5 copy-start.1
  182.4 2.2 copy-start
  189.1 14.2 %collective-permute-start = (bf16[32,8192]{1,0:T(8,128)(2,1)S(1)}, bf16[32,8192]{1,0:T(8,128)(2,1)S(1)}, u32[]{:S(2)}, u32[]{:S(2)}) collective-permute-start(bf16[32,8192]{1,0:T(8,128)(2,1)S(1)} %get-tuple-element.590), channel_id=1, source_target_pairs={{16,0},{17,1},{18,2},{19,3},{20,4},{21,5},{22,6},{23,7},{24,8},{25... | collective-permute-start | bytes 1572872 | tf_op jit(solution)/shard_map/while/body/eval_jaxpr/ppermute | solution.py:15
  203.6 3.5 copy-start.1
  209.5 2.2 copy-start
  216.2 13.3 %collective-permute-start = (bf16[32,8192]{1,0:T(8,128)(2,1)S(1)}, bf16[32,8192]{1,0:T(8,128)(2,1)S(1)}, u32[]{:S(2)}, u32[]{:S(2)}) collective-permute-start(bf16[32,8192]{1,0:T(8,128)(2,1)S(1)} %get-tuple-element.590), channel_id=1, source_target_pairs={{16,0},{17,1},{18,2},{19,3},{20,4},{21,5},{22,6},{23,7},{24,8},{25... | collective-permute-start | bytes 1572872 | tf_op jit(solution)/shard_map/while/body/eval_jaxpr/ppermute | solution.py:15
  229.8 3.5 copy-start.1
  235.7 2.2 copy-start
  242.4 12.4 %collective-permute-start = (bf16[32,8192]{1,0:T(8,128)(2,1)S(1)}, bf16[32,8192]{1,0:T(8,128)(2,1)S(1)}, u32[]{:S(2)}, u32[]{:S(2)}) collective-permute-start(bf16[32,8192]{1,0:T(8,128)(2,1)S(1)} %get-tuple-element.590), channel_id=1, source_target_pairs={{16,0},{17,1},{18,2},{19,3},{20,4},{21,5},{22,6},{23,7},{24,8},{25... | collective-permute-start | bytes 1572872 | tf_op jit(solution)/shard_map/while/body/eval_jaxpr/ppermute | solution.py:15
  254.8 5.0 %copy-start.3 = (bf16[128,8192]{1,0:T(8,128)(2,1)S(1)}, bf16[128,8192]{1,0:T(8,128)(2,1)}, u32[]{:S(2)}) copy-start(bf16[128,8192]{1,0:T(8,128)(2,1)} %get-tuple-element.371) | copy-start | bytes 6291460
  270.7 0.7 copy-start.6
Sparse Core Ops, SparseCore 0:
  10.2 53.2 all-gather.4
  65.6 49.0 all-gather.6
  270.8 102.6 reduce-scatter.1
where the time goes:
time: 384 us; the launch traced here: 383 us
  waiting for transfers between devices  212 us (55%)
  blocking collectives  59.9 us (16%)
  matrix products  47.9 us (12%)
  other arithmetic  26.3 us (7%)
  local copies, waits for them, and re-layouts  15.7 us (4%)
  between operations  14.5 us (4%)
  starting transfers between devices  6.52 us (2%)
    ppermute x5, waiting for transfers between devices, shifted(): return lax.ppermute(block, axis, route)  64.5 us
    unnamed x1, blocking collectives  59.9 us
    all_gather x1, waiting for transfers between devices, local(): lax.all_gather(w_down[0], 'dp', axis=0, tiled=True)  54.7 us
    all_gather x1, waiting for transfers between devices, local(): lax.all_gather(w_up[0], 'dp', axis=0, tiled=True)  51.2 us
    reduce_scatter x1, waiting for transfers between devices, local(): lax.psum_scatter(jnp.concatenate([down_part, up_part], axis=1).astype(jnp...  40.4 us
    dot_general x5, matrix products, run_step(): preact = jnp.dot(scaled, down_matrix, preferred_element_type=jnp.float32)  16.2 us
    dynamic_update_slice x5, other arithmetic, write_rows(): lax.dynamic_update_slice_in_dim(buffer, jnp.where(active_step, fresh, pre...  15.1 us
    dot_general x5, matrix products, run_step(): jnp.einsum('tr,dr->td', hidden, up_matrix, preferred_element_type=jnp.flo...  12 us
  transfers between devices with their start and end apart: 8, of which 8 were waited for; matrix products, arithmetic and copies ran while one was open for 0% of the time, Pallas kernels for 0%

commit v1 on v0

--- a/solution.py
+++ b/solution.py
@@ -2,11 +2,40 @@
 import jax.numpy as jnp
 from jax import lax
 from jax.sharding import PartitionSpec as P
+from jax.lax import axis_index, axis_size, ppermute
 
 MICRO = 4
 ROWS = 32
 TOK_DEV = 128
 EPSILON = 1e-05
+
+
+def take_steps_all_for(patch, array_dim):
+    patch = jnp.moveaxis(patch, 0, array_dim)
+    reached = patch.shape
+    step_out = patch.reshape(
+        *reached[:array_dim], reached[array_dim] * reached[array_dim + 1], *reached[array_dim + 2 :]
+    )
+    return step_out
+
+
+def hubs_place(u_in, device_axis):
+    lanes = axis_size(device_axis)
+    n_now = u_in[None]
+    for rr in range(lanes.bit_length() - 1):
+        field_out = 1 << rr
+        base_arr = ppermute(
+            n_now, device_axis, list(map(lambda m: (m, m ^ field_out), range(lanes)))
+        )
+        before = jnp.stack([n_now, base_arr])
+        t_next = axis_index(device_axis) >> rr & 1
+        n_now = jnp.where(t_next == 0, before, before[::-1]).reshape(-1, *u_in.shape)
+    return n_now
+
+
+def work_widths(block_here, u, d_out):
+    e_now = take_steps_all_for(hubs_place(block_here, u), d_out)
+    return e_now
 
 
 def shifted(block, axis, distance):
@@ -29,7 +58,7 @@
     gain = gains[0]
     down_matrix, up_matrix = (
         lax.all_gather(w_down[0], "dp", axis=0, tiled=True),
-        lax.all_gather(w_up[0], "dp", axis=0, tiled=True),
+        work_widths(w_up[0], "dp", 0),
     )
     is_last = section_index == sections - 1
     rank_width = down_matrix.shape[1]

time: 384 us -> 442 us (1.15)
  waiting for transfers between devices: 212 us -> 257 us
  other arithmetic: 26.3 us -> 33.3 us
  starting transfers between devices: 6.52 us -> 12.5 us
    ppermute x0 -> x4, waiting for transfers between devices: none -> 152 us  [hubs_place(): ppermute(n_now, device_axis, list(map(lambda m: (m, m ^ field_out), range...]
    all_gather x1, waiting for transfers between devices: 54.7 us -> 0.01 us  [local(): lax.all_gather(w_down[0], 'dp', axis=0, tiled=True)]
    all_gather x1 -> x0, waiting for transfers between devices: 51.2 us -> none  [local(): lax.all_gather(w_up[0], 'dp', axis=0, tiled=True)]
    ppermute x0 -> x4, starting transfers between devices: none -> 6.04 us  [hubs_place(): ppermute(n_now, device_axis, list(map(lambda m: (m, m ^ field_out), range...]
  transfers between devices with their start and end apart: 8 -> 11, of which waited for: 8 -> 10; matrix products, arithmetic and copies ran while one was open for 0% -> 2% of each run, Pallas kernels for 0% -> 0%
where the time goes in v1:
time: 442 us; the launch traced here: 441 us
  waiting for transfers between devices  257 us (58%)
  blocking collectives  59.5 us (13%)
  matrix products  47.9 us (11%)
  other arithmetic  33.3 us (8%)
  local copies, waits for them, and re-layouts  15.7 us (4%)
  between operations  14.8 us (3%)
  starting transfers between devices  12.5 us (3%)
    ppermute x4, waiting for transfers between devices, hubs_place(): ppermute(n_now, device_axis, list(map(lambda m: (m, m ^ field_out), range...  152 us
    ppermute x5, waiting for transfers between devices, shifted(): return lax.ppermute(block, axis, route)  62.9 us
    unnamed x1, blocking collectives  59.5 us
    reduce_scatter x1, waiting for transfers between devices, local(): lax.psum_scatter(jnp.concatenate([down_part, up_part], axis=1).astype(jnp...  41.4 us
    dot_general x5, matrix products, run_step(): preact = jnp.dot(scaled, down_matrix, preferred_element_type=jnp.float32)  16.2 us
    dynamic_update_slice x5, other arithmetic, write_rows(): lax.dynamic_update_slice_in_dim(buffer, jnp.where(active_step, fresh, pre...  15.1 us
    dot_general x5, matrix products, run_step(): jnp.einsum('tr,dr->td', hidden, up_matrix, preferred_element_type=jnp.flo...  12 us
  transfers between devices with their start and end apart: 11, of which 10 were waited for; matrix products, arithmetic and copies ran while one was open for 2% of the time, Pallas kernels for 0%

profile of v1, /device:TPU:0, one launch (start us, length us, event | category | flops | bytes accessed | tf_op | source)
XLA Modules:
  0.0 440.8 jit_solution(8160343938024361907)
XLA Ops:
  8.5 1.4 collective-permute-done.1
  11.0 3.0 collective-permute-start.2
  13.9 15.0 %collective-permute-done.2 = bf16[2,512,256]{2,1,0:T(8,128)(2,1)S(1)} collective-permute-done((bf16[2,512,256]{2,1,0:T(8,128)(2,1)S(1)}, bf16[2,512,256]{2,1,0:T(8,128)(2,1)S(1)}, u32[]{:S(2)}, u32[]{:S(2)}) %collective-permute-start.2) | collective-permute-done | bytes 524320 | tf_op jit(solution)/shard_map/ppermute | solution.py:27
  29.3 1.9 collective-permute-start.3
  31.1 43.2 %collective-permute-done.3 = bf16[4,512,256]{2,1,0:T(8,128)(2,1)S(1)} collective-permute-done((bf16[4,512,256]{2,1,0:T(8,128)(2,1)S(1)}, bf16[4,512,256]{2,1,0:T(8,128)(2,1)S(1)}, u32[]{:S(2)}, u32[]{:S(2)}) %collective-permute-start.3) | collective-permute-done | bytes 1048608 | tf_op jit(solution)/shard_map/ppermute | solution.py:27
  75.7 92.3 %collective-permute-done.4 = bf16[8,512,256]{2,1,0:T(8,128)(2,1)} collective-permute-done((bf16[8,512,256]{2,1,0:T(8,128)(2,1)S(1)}, bf16[8,512,256]{2,1,0:T(8,128)(2,1)}, u32[]{:S(2)}, u32[]{:S(2)}) %collective-permute-start.4) | collective-permute-done | bytes 2097184 | tf_op jit(solution)/shard_map/ppermute | solution.py:27
  168.0 2.0 pad_maximum_fusion.1
  170.0 3.0 reverse_select_fusion
  173.0 1.5 broadcast.67.clone.1
  174.5 1.5 broadcast.67.clone
  176.1 1.5 broadcast.67
  177.6 133.8 %while.28 = (s32[]{:T(128)}, bf16[32,8192]{1,0:T(8,128)(2,1)S(1)}, bf16[128,8192]{1,0:T(8,128)(2,1)}, bf16[128,8192]{1,0:T(8,128)(2,1)}, bf16[128,256]{1,0:T(8,1...) while((s32[]{:T(128)}, bf16[32,8192]{1,0:T(8,128)(2,1)S(1)}, ...), condition=%wide.region_4.5_spmd.clone, body=%wide.region_0.4_spmd.clone.sunk | while | flops 546234496 | bytes 63868848 | solution.py:120
  178.0 3.2 select_dynamic-update-slice_fusion.8
  181.4 2.4 fusion.50
  184.7 1.3 copy-done.1
  186.0 1.5 fusion.51
  187.5 3.0 select_dynamic-update-slice_fusion.10
  190.5 1.3 collective-permute-start
  191.8 14.4 %collective-permute-done = bf16[32,8192]{1,0:T(8,128)(2,1)S(1)} collective-permute-done((bf16[32,8192]{1,0:T(8,128)(2,1)S(1)}, bf16[32,8192]{1,0:T(8,128)(2,1)S(1)}, u32[]{:S(2)}, u32[]{:S(2)}) %collective-permute-start) | collective-permute-done | bytes 524320 | tf_op jit(solution)/shard_map/while/body/eval_jaxpr/ppermute | solution.py:44
  206.5 3.2 select_dynamic-update-slice_fusion.8
  210.0 2.4 fusion.50
  213.2 1.3 copy-done.1
  214.6 1.5 fusion.51
  216.0 3.0 select_dynamic-update-slice_fusion.10
  220.4 13.5 %collective-permute-done = bf16[32,8192]{1,0:T(8,128)(2,1)S(1)} collective-permute-done((bf16[32,8192]{1,0:T(8,128)(2,1)S(1)}, bf16[32,8192]{1,0:T(8,128)(2,1)S(1)}, u32[]{:S(2)}, u32[]{:S(2)}) %collective-permute-start) | collective-permute-done | bytes 524320 | tf_op jit(solution)/shard_map/while/body/eval_jaxpr/ppermute | solution.py:44
  234.2 3.2 select_dynamic-update-slice_fusion.8
  237.7 2.4 fusion.50
  240.9 1.3 copy-done.1
  242.3 1.5 fusion.51
  243.7 3.0 select_dynamic-update-slice_fusion.10
  248.1 12.6 %collective-permute-done = bf16[32,8192]{1,0:T(8,128)(2,1)S(1)} collective-permute-done((bf16[32,8192]{1,0:T(8,128)(2,1)S(1)}, bf16[32,8192]{1,0:T(8,128)(2,1)S(1)}, u32[]{:S(2)}, u32[]{:S(2)}) %collective-permute-start) | collective-permute-done | bytes 524320 | tf_op jit(solution)/shard_map/while/body/eval_jaxpr/ppermute | solution.py:44
  261.0 3.2 select_dynamic-update-slice_fusion.8
  264.4 2.4 fusion.50
  267.7 1.3 copy-done.1
  269.0 1.5 fusion.51
  270.5 3.0 select_dynamic-update-slice_fusion.10
  274.8 11.7 %collective-permute-done = bf16[32,8192]{1,0:T(8,128)(2,1)S(1)} collective-permute-done((bf16[32,8192]{1,0:T(8,128)(2,1)S(1)}, bf16[32,8192]{1,0:T(8,128)(2,1)S(1)}, u32[]{:S(2)}, u32[]{:S(2)}) %collective-permute-start) | collective-permute-done | bytes 524320 | tf_op jit(solution)/shard_map/while/body/eval_jaxpr/ppermute | solution.py:44
  286.8 3.2 select_dynamic-update-slice_fusion.8
  290.3 2.4 fusion.50
  293.5 1.3 copy-done.1
  294.9 1.5 fusion.51
  296.4 3.0 select_dynamic-update-slice_fusion.10
  300.7 10.7 %collective-permute-done = bf16[32,8192]{1,0:T(8,128)(2,1)S(1)} collective-permute-done((bf16[32,8192]{1,0:T(8,128)(2,1)S(1)}, bf16[32,8192]{1,0:T(8,128)(2,1)S(1)}, u32[]{:S(2)}, u32[]{:S(2)}) %collective-permute-start) | collective-permute-done | bytes 524320 | tf_op jit(solution)/shard_map/while/body/eval_jaxpr/ppermute | solution.py:44
  311.4 5.0 %convolution_convert_fusion.1 = bf16[8192,256]{0,1:T(8,128)(2,1)} fusion(bf16[128,8192]{1,0:T(8,128)(2,1)} %get-tuple-element.369, bf16[128,256]{1,0:T(8,128)(2,1)S(1)} %get-tuple-element.370), kind=kOutput, calls=%fused_computation.36 | convolution fusion | flops 538968064 | bytes 6356992 | tf_op jit(solution)/shard_map/td,tr->dr/dot_general | solution.py:122
  316.4 3.2 convolution_convert_fusion
  319.6 7.7 %pad_maximum_fusion = bf16[8192,512]{0,1:T(8,128)(2,1)} fusion(bf16[8192,256]{0,1:T(8,128)(2,1)} %convolution_convert_fusion, bf16[8192,256]{0,1:T(8,128)(2,1)} %convolution_convert_fusion.1), kind=kLoop, calls=%fused_computation.37 | loop fusion | flops 16777216 | bytes 16777216 | tf_op jit(solution)/shard_map/concatenate | solution.py:125
  329.2 59.5 %all-reduce = f32[8192]{0:T(1024)S(1)} all-reduce(f32[8192]{0:T(1024)S(1)} %get-tuple-element.373), channel_id=4, replica_groups=mesh['section'=2,'dp'=16] {'dp'}, use_global_device_ids=true, to_apply=%region_6.7.clone | all-reduce | flops 8192 | bytes 65536
  389.4 41.4 %reduce-scatter.2.cloned.1.call-done = bf16[512,512]{0,1:T(8,128)(2,1)} async-done(((bf16[8192,512]{0,1:T(8,128)(2,1)}), bf16[512,512]{0,1:T(8,128)(2,1)}) %reduce-scatter.2.cloned.1.call-update) | async-done | bytes 524304 | tf_op jit(solution)/shard_map/reduce_scatter | solution.py:124
  (82 shorter events, 21.2 us)
Async XLA Ops:
  7.2 165.8 %all-gather.3.cloned.1.call-start = ((), (), s32[]{:S(2)}) async-start(), calls=%async_computation.2 | async-start | bytes 4456448 | tf_op jit(solution)/shard_map/all_gather | solution.py:60
  7.9 422.8 %reduce-scatter.2.cloned.1.call-start = ((), (), s32[]{:S(2)}) async-start(), calls=%async_computation.1 | async-start | bytes 8912896 | tf_op jit(solution)/shard_map/reduce_scatter | solution.py:124
  7.9 1.9 collective-permute-start.1
  11.0 18.0 %collective-permute-start.2 = (bf16[2,512,256]{2,1,0:T(8,128)(2,1)S(1)}, bf16[2,512,256]{2,1,0:T(8,128)(2,1)S(1)}, u32[]{:S(2)}, u32[]{:S(2)}) collective-permute-start(bf16[2,512,256]{2,1,0:T(8,128)(2,1)S(1)} %get-tuple-element.479), channel_id=1, source_target_pairs={{0,2},{1,3},{2,0},{3,1},{4,6},{5,7},{6,4},{7,5},{8,10},{9,11},{10,... | collective-permute-start | bytes 1572872 | tf_op jit(solution)/shard_map/ppermute | solution.py:27
  29.3 45.1 %collective-permute-start.3 = (bf16[4,512,256]{2,1,0:T(8,128)(2,1)S(1)}, bf16[4,512,256]{2,1,0:T(8,128)(2,1)S(1)}, u32[]{:S(2)}, u32[]{:S(2)}) collective-permute-start(bf16[4,512,256]{2,1,0:T(8,128)(2,1)S(1)} %bitcast.57), channel_id=1, source_target_pairs={{0,4},{1,5},{2,6},{3,7},{4,0},{5,1},{6,2},{7,3},{8,12},{9,13},{10,... | collective-permute-start | bytes 3145736 | tf_op jit(solution)/shard_map/ppermute | solution.py:27
  75.0 93.0 %collective-permute-start.4 = (bf16[8,512,256]{2,1,0:T(8,128)(2,1)S(1)}, bf16[8,512,256]{2,1,0:T(8,128)(2,1)}, u32[]{:S(2)}, u32[]{:S(2)}) collective-permute-start(bf16[8,512,256]{2,1,0:T(8,128)(2,1)S(1)} %bitcast.52), channel_id=1, source_target_pairs={{0,8},{1,9},{2,10},{3,11},{4,12},{5,13},{6,14},{7,15},{8,0},{9,1},... | collective-permute-start | bytes 6291464 | tf_op jit(solution)/shard_map/ppermute | solution.py:27
  174.5 3.0 copy-start.2
  174.5 3.0 copy-start.4
  174.5 3.0 copy-start.5
  177.9 3.5 copy-start
  183.8 2.2 copy-start.1
  190.5 15.7 %collective-permute-start = (bf16[32,8192]{1,0:T(8,128)(2,1)S(1)}, bf16[32,8192]{1,0:T(8,128)(2,1)S(1)}, u32[]{:S(2)}, u32[]{:S(2)}) collective-permute-start(bf16[32,8192]{1,0:T(8,128)(2,1)S(1)} %get-tuple-element.592), channel_id=1, source_target_pairs={{16,0},{17,1},{18,2},{19,3},{20,4},{21,5},{22,6},{23,7},{24,8},{25... | collective-permute-start | bytes 1572872 | tf_op jit(solution)/shard_map/while/body/eval_jaxpr/ppermute | solution.py:44
  206.5 3.5 copy-start
  212.4 2.2 copy-start.1
  219.0 14.8 %collective-permute-start = (bf16[32,8192]{1,0:T(8,128)(2,1)S(1)}, bf16[32,8192]{1,0:T(8,128)(2,1)S(1)}, u32[]{:S(2)}, u32[]{:S(2)}) collective-permute-start(bf16[32,8192]{1,0:T(8,128)(2,1)S(1)} %get-tuple-element.592), channel_id=1, source_target_pairs={{16,0},{17,1},{18,2},{19,3},{20,4},{21,5},{22,6},{23,7},{24,8},{25... | collective-permute-start | bytes 1572872 | tf_op jit(solution)/shard_map/while/body/eval_jaxpr/ppermute | solution.py:44
  234.2 3.5 copy-start
  240.1 2.2 copy-start.1
  246.7 13.9 %collective-permute-start = (bf16[32,8192]{1,0:T(8,128)(2,1)S(1)}, bf16[32,8192]{1,0:T(8,128)(2,1)S(1)}, u32[]{:S(2)}, u32[]{:S(2)}) collective-permute-start(bf16[32,8192]{1,0:T(8,128)(2,1)S(1)} %get-tuple-element.592), channel_id=1, source_target_pairs={{16,0},{17,1},{18,2},{19,3},{20,4},{21,5},{22,6},{23,7},{24,8},{25... | collective-permute-start | bytes 1572872 | tf_op jit(solution)/shard_map/while/body/eval_jaxpr/ppermute | solution.py:44
  261.0 3.5 copy-start
  266.8 2.2 copy-start.1
  273.5 13.0 %collective-permute-start = (bf16[32,8192]{1,0:T(8,128)(2,1)S(1)}, bf16[32,8192]{1,0:T(8,128)(2,1)S(1)}, u32[]{:S(2)}, u32[]{:S(2)}) collective-permute-start(bf16[32,8192]{1,0:T(8,128)(2,1)S(1)} %get-tuple-element.592), channel_id=1, source_target_pairs={{16,0},{17,1},{18,2},{19,3},{20,4},{21,5},{22,6},{23,7},{24,8},{25... | collective-permute-start | bytes 1572872 | tf_op jit(solution)/shard_map/while/body/eval_jaxpr/ppermute | solution.py:44
  286.8 3.5 copy-start
  292.7 2.2 copy-start.1
  299.4 12.1 %collective-permute-start = (bf16[32,8192]{1,0:T(8,128)(2,1)S(1)}, bf16[32,8192]{1,0:T(8,128)(2,1)S(1)}, u32[]{:S(2)}, u32[]{:S(2)}) collective-permute-start(bf16[32,8192]{1,0:T(8,128)(2,1)S(1)} %get-tuple-element.592), channel_id=1, source_target_pairs={{16,0},{17,1},{18,2},{19,3},{20,4},{21,5},{22,6},{23,7},{24,8},{25... | collective-permute-start | bytes 1572872 | tf_op jit(solution)/shard_map/while/body/eval_jaxpr/ppermute | solution.py:44
  311.4 5.0 %copy-start.3 = (bf16[128,8192]{1,0:T(8,128)(2,1)S(1)}, bf16[128,8192]{1,0:T(8,128)(2,1)}, u32[]{:S(2)}) copy-start(bf16[128,8192]{1,0:T(8,128)(2,1)} %get-tuple-element.371) | copy-start | bytes 6291460
  327.3 0.7 copy-start.6
Sparse Core Ops, SparseCore 0:
  10.2 64.7 all-gather.2
  327.5 103.2 reduce-scatter.1
